TPU v7x, 128 devices: a whole 4x4x4 slice. The times are simulated.
128 devices in a mesh: aux: 4 (over x_lo, core), ao: 32 (over z, y, x_hi).
Axes of the slice: x: 4 (x_hi: 2, x_lo: 2; x = x_hi * 2 + x_lo), y: 4, z: 4, core: 2. Of those that a mesh axis runs over, the one named last changes fastest.
Arguments:
- cholesky: bfloat16 [64, 4096, 4096], P('aux', 'ao'), may hold values from -3.5 to 3.5, as said below
- coeffs: bfloat16 [4096, 128], P('ao'), may hold values from -0.09375 to 0.09375
Outputs:
- integrals: float32 [16384, 16384], P('aux', 'ao')
Inputs may be any that keep to these rules, and one draw needn't show every extreme that they name: cholesky[L, mu, nu] = cholesky[L, nu, mu] for every vector L.
All inputs are finite; a program needn't handle non-finite values.
Results may differ from a plain program's by a relative error of at most 0.0091.
Values may be sent and summed in bfloat16 or wider, within the bound.
No kernel may reach another device: no remote copies, remote signals or barrier semaphores. Data moves between devices by JAX's collectives and lax.ppermute only.
A program may use at most 64 MiB of HBM per device.

v0:
```python
import jax
import jax.numpy as jnp
from jax import lax
from jax.sharding import PartitionSpec as P


def laid_out(blocks, dim):
    dims = list(blocks.shape[1:])
    dims[dim] *= blocks.shape[0]
    return jnp.moveaxis(blocks, 0, dim).reshape(dims)


def from_everyone(value, axis):
    copies = jnp.broadcast_to(value, (lax.axis_size(axis), *value.shape))
    return lax.all_to_all(copies, axis, split_axis=0, concat_axis=0, tiled=True)


def gather_directly(value, axis, dim):
    return laid_out(from_everyone(value, axis), dim)


def cut_along(value, dim, size):
    dims = value.shape
    blocks = value.reshape(*dims[:dim], size, dims[dim] // size, *dims[dim + 1 :])
    return jnp.moveaxis(blocks, dim, 0)


def sum_at_owner(value, axis, dim):
    blocks = cut_along(value, dim, lax.axis_size(axis))
    arrived = lax.all_to_all(blocks, axis, split_axis=0, concat_axis=0, tiled=True)
    return arrived.astype(jnp.float32).sum(axis=0)


def on_device(cholesky, coeffs):
    nvec_here, row_count, basis = cholesky.shape
    active = coeffs.shape[1]
    flat_rows = cholesky.reshape(nvec_here * row_count, basis)
    half = jnp.dot(flat_rows, gather_directly(coeffs, "ao", 0), preferred_element_type=jnp.float32)
    half = half.astype(jnp.bfloat16).reshape(nvec_here, row_count, active)
    partial_value = jnp.einsum("mi,lmj->lij", coeffs, half, preferred_element_type=jnp.float32)
    width = active // lax.axis_size("ao")
    mine = sum_at_owner(partial_value.astype(jnp.bfloat16), "ao", 1).astype(jnp.bfloat16)
    complete = gather_directly(mine, "ao", 1)
    band = active // lax.axis_size("aux")
    every_vector = gather_directly(complete, "aux", 0)
    every_rows = lax.dynamic_slice_in_dim(every_vector, lax.axis_index("aux") * band, band, 1)
    every_cols = lax.dynamic_slice_in_dim(every_vector, lax.axis_index("ao") * width, width, 1)
    left = every_rows.reshape(every_rows.shape[0], band * active)
    right = every_cols.reshape(every_cols.shape[0], width * active)
    return lax.dot_general(
        left, right, (((0,), (0,)), ((), ())), preferred_element_type=jnp.float32
    )


def solution(mesh):
    in_specs = (P("aux", "ao", None), P("ao", None))
    out_specs = P("aux", "ao")
    return jax.shard_map(
        on_device, mesh=mesh, in_specs=in_specs, out_specs=out_specs, check_vma=False
    )
```

profile of v0, /device:TPU:1, one launch (start us, length us, event | category | flops | bytes accessed | tf_op | source)
XLA Modules:
  0.0 108.7 jit_solution(17526252577135699135)
XLA Ops:
  0.0 1.0 broadcast_in_dim.9
  1.0 29.3 %all_to_all.20 = bf16[32,128,128]{2,1,0:T(8,128)(2,1)S(1)} all-to-all(bf16[32,128,128]{2,1,0:T(8,128)(2,1)S(1)} %broadcast_in_dim.9), channel_id=1, replica_groups=mesh['aux'=4,'ao'=32] {'ao'}, dimensions={0} | all-to-all | bytes 2097152 | tf_op jit(solution)/shard_map/all_to_all | solution.py:15
  30.3 0.0 copy-start
  30.3 8.2 %convolution_convert_fusion = bf16[2048,128]{1,0:T(8,128)(2,1)S(1)} fusion(bf16[2048,4096]{1,0:T(8,128)(2,1)} %bitcast.36, bf16[4096,128]{1,0:T(8,128)(2,1)S(1)} %bitcast.33), kind=kOutput, calls=%fused_computation | convolution fusion | flops 2147745792 | bytes 18350080 | tf_op jit(solution)/shard_map/dot_general | solution.py:38
  38.5 0.0 copy-done
  38.5 0.3 convolution_convert_fusion.1
  38.8 0.3 copy.25
  39.1 14.8 %all_to_all.21 = bf16[32,16,4,128]{3,2,1,0:T(4,128)(2,1)S(1)} all-to-all(bf16[32,16,4,128]{3,2,1,0:T(4,128)(2,1)S(1)} %bitcast.31), channel_id=1, replica_groups=mesh['aux'=4,'ao'=32] {'ao'}, dimensions={0} | all-to-all | bytes 1048576 | tf_op jit(solution)/shard_map/all_to_all | solution.py:30
  53.9 0.2 reduce_sum.12
  54.1 0.1 broadcast_in_dim.10
  54.3 14.8 %all_to_all.22 = bf16[32,16,4,128]{3,1,2,0:T(8,128)(2,1)S(1)} all-to-all(bf16[32,16,4,128]{3,1,2,0:T(8,128)(2,1)S(1)} %broadcast_in_dim.10), channel_id=1, replica_groups=mesh['aux'=4,'ao'=32] {'ao'}, dimensions={0} | all-to-all | bytes 1048576 | tf_op jit(solution)/shard_map/all_to_all | solution.py:15
  69.1 0.1 copy.10
  69.2 1.9 %broadcast_in_dim.11 = bf16[4,16,128,128]{3,2,1,0:T(8,128)(2,1)} broadcast(bf16[16,128,128]{2,1,0:T(8,128)(2,1)S(1)} %copy.10), dimensions={1,2,3} | broadcast | bytes 2621440 | tf_op jit(solution)/shard_map/broadcast_in_dim | solution.py:14
  71.1 8.0 %all-to-all-start.3 = ((bf16[4,16,128,128]{3,2,1,0:T(8,128)(2,1)}), bf16[4,16,128,128]{3,2,1,0:T(8,128)(2,1)S(1)}, u32[]{:S(2)}, u32[]{:S(2)}) async-start(bf16[4,16,128,128]{3,2,1,0:T(8,128)(2,1)} %broadcast_in_dim.11), calls=%async_computation.3 | async-start | bytes 4194304 | tf_op jit(solution)/shard_map/all_to_all | solution.py:15
  79.1 24.8 %all-to-all-done.3 = bf16[4,16,128,128]{3,2,1,0:T(8,128)(2,1)S(1)} async-done(((bf16[4,16,128,128]{3,2,1,0:T(8,128)(2,1)}), bf16[4,16,128,128]{3,2,1,0:T(8,128)(2,1)S(1)}, u32[]{:S(2)}, u32[]{:S(2)}) %all-to-all-start.3) | async-done | bytes 2097184 | tf_op jit(solution)/shard_map/all_to_all | solution.py:15
  104.0 4.7 %fusion = f32[4096,512]{1,0:T(8,128)} fusion(bf16[8,8,32,128]{3,2,1,0:T(8,128)(2,1)S(1)} %bitcast.27, bf16[8,8,4,128]{3,2,1,0:T(4,128)(2,1)S(1)} %bitcast.35), kind=kOutput, calls=%fused_computation.2 | convolution fusion | flops 268435456 | bytes 8978432 | tf_op jit(solution)/shard_map/dot_general | solution.py:50
  (3 shorter events, 0.1 us)
Async XLA Ops:
  30.3 8.2 %copy-start = (bf16[128,128]{1,0:T(8,128)(2,1)S(1)}, bf16[128,128]{1,0:T(8,128)(2,1)}, u32[]{:S(2)}) copy-start(bf16[128,128]{1,0:T(8,128)(2,1)} %param.3) | copy-start | bytes 98308
  71.1 32.8 %all-to-all-start.3 = ((bf16[4,16,128,128]{3,2,1,0:T(8,128)(2,1)}), bf16[4,16,128,128]{3,2,1,0:T(8,128)(2,1)S(1)}, u32[]{:S(2)}, u32[]{:S(2)}) async-start(bf16[4,16,128,128]{3,2,1,0:T(8,128)(2,1)} %broadcast_in_dim.11), calls=%async_computation.3 | async-start | bytes 4194304 | tf_op jit(solution)/shard_map/all_to_all | solution.py:15
where the time goes:
time: 109 us
  blocking collectives  58.9 us (54%)
  waiting for transfers between devices  24.8 us (23%)
  matrix products  13.2 us (12%)
  starting transfers between devices  7.97 us (7%)
  local copies, waits for them, and re-layouts  3.48 us (3%)
    all_to_all x2, blocking collectives, from_everyone(): return lax.all_to_all(copies, axis, split_axis=0, concat_axis=0, tiled=True)  44.1 us
    all_to_all x1, waiting for transfers between devices, from_everyone(): return lax.all_to_all(copies, axis, split_axis=0, concat_axis=0, tiled=True)  24.8 us
    all_to_all x1, blocking collectives, sum_at_owner(): lax.all_to_all(blocks, axis, split_axis=0, concat_axis=0, tiled=True)  14.8 us
    dot_general x1, matrix products, on_device(): jnp.dot(flat_rows, gather_directly(coeffs, 'ao', 0), preferred_element_ty...  8.19 us
    all_to_all x1, starting transfers between devices, from_everyone(): return lax.all_to_all(copies, axis, split_axis=0, concat_axis=0, tiled=True)  7.97 us
    dot_general x1, matrix products, on_device(): lax.dot_general(left, right, (((0,), (0,)), ((), ())), preferred_element_...  4.68 us
    broadcast_in_dim x3, local copies, waits for them, and re-layouts, from_everyone(): copies = jnp.broadcast_to(value, (lax.axis_size(axis), *value.shape))  2.98 us
  transfers between devices with their start and end apart: 1, of which 1 were waited for; matrix products, arithmetic and copies ran while one was open for 0% of the time, Pallas kernels for 0%

commit v1 on v0

v1 whole, which is shorter than its diff:
```python
import jax
import jax.numpy as jnp
from jax import lax
from jax.experimental import pallas as pl
from jax.experimental.pallas import tpu as pltpu
from jax.sharding import PartitionSpec as P

BF16, F32 = jnp.bfloat16, jnp.float32
VMEM = pl.BlockSpec(memory_space=pltpu.VMEM)
ANY = pl.BlockSpec(memory_space=pl.ANY)


def exchange(blocks, axes):
    return lax.all_to_all(blocks, axes, split_axis=0, concat_axis=0, tiled=True)


def start_window(chol_ref, held_ref, sem):
    span = held_ref.shape[2]
    wide = 2 * held_ref.shape[1]
    wides = chol_ref.shape[2] // wide
    at = lax.axis_index("ao") // 2

    def start(source, target, size):
        pltpu.make_async_copy(
            chol_ref.at[:, :, pl.ds(source, size)], held_ref.at[:, :, pl.ds(target, size)], sem
        ).start()

    for c in range(wides):

        @pl.when(at == c)
        def _(c=c):
            ahead = min(span, (wides - c) * wide)
            start(c * wide, 0, ahead)
            if ahead < span:
                start(0, ahead, span - ahead)


def wait_window(held_ref, sem):
    pltpu.make_async_copy(held_ref, held_ref, sem).wait()


def fetch(chol_ref, out_ref, sem):
    start_window(chol_ref.at[pl.ds(0, out_ref.shape[0])], out_ref, sem)
    wait_window(out_ref, sem)


def pair_sums(
    early_ref, chol_ref, mine_ref, other_ref, coeffs_ref, out_ref, held_ref, near_ref, sems, *, step
):
    ready, rows, span = early_ref.shape
    nvec = ready + held_ref.shape[0]
    blocks, part, active = mine_ref.shape
    wide = 2 * rows
    steps, wides = span // wide, blocks // 2
    core, at = lax.axis_index("aux") % 2, lax.axis_index("ao") // 2

    def late(first):
        return held_ref.at[pl.ds(first - ready, step)]

    for first in range(ready, nvec, step):
        start_window(chol_ref.at[pl.ds(first, step)], late(first), sems.at[first // step])
    for t in range(steps):
        for s in range(2):
            block = lax.rem(at + t, wides) * 2 + s
            for ref, half in ((mine_ref, core), (other_ref, 1 - core)):
                value = ref[block]
                if t in (0, steps - 1):
                    value = value * BF16(0.5)
                where = wide * t + rows * s + half * part
                near_ref[pl.ds(pl.multiple_of(where, part), part), :] = value
    near = near_ref[...]
    turned = coeffs_ref[...].astype(F32).T.astype(BF16)

    def finish(first, half):
        half = jnp.concatenate([half[v * rows : (v + 1) * rows] for v in range(step)], axis=1)
        sums = jnp.dot(turned, half, preferred_element_type=F32)
        for v in range(step):
            one = sums[:, v * active : (v + 1) * active]
            out_ref[first + v] = (one + one.T).astype(BF16)

    before = None
    for first in range(0, nvec, step):
        if first < ready:
            slab = early_ref[first : first + step]
        else:
            wait_window(late(first), sems.at[first // step])
            slab = late(first)[...]
        slab = slab.reshape(step * rows, span)
        half = jnp.dot(slab, near, preferred_element_type=F32).astype(BF16)
        if before is not None:
            finish(*before)
        before = first, half
    finish(*before)


def products(left_ref, right_ref, out_ref):
    auxes, count, deep, active = left_ref.shape
    nvec = right_ref.shape[0] // auxes
    for k in range(count):
        left = jnp.concatenate([left_ref[a, k, :nvec, :] for a in range(auxes)], axis=0)
        out_ref[k * active : (k + 1) * active, :] = lax.dot_general(
            left, right_ref[...], (((0,), (0,)), ((), ())), preferred_element_type=F32
        )


def on_device(cholesky, coeffs):
    nvec, rows, basis = cholesky.shape
    active = coeffs.shape[1]
    auxes, aos = lax.axis_size("aux"), lax.axis_size("ao")
    band, width = active // auxes, active // aos
    core = lax.axis_index("aux") % 2

    own = lax.dynamic_slice_in_dim(coeffs, core * (rows // 2), rows // 2, 0)
    mine = exchange(jnp.broadcast_to(own, (aos, rows // 2, active)), "ao")
    other = lax.ppermute(mine, "aux", [(a, a ^ 1) for a in range(auxes)])
    span, ready, step = (aos // 4 + 1) * 2 * rows, nvec // 2, 2
    early = pl.pallas_call(
        fetch,
        out_shape=jax.ShapeDtypeStruct((ready, rows, span), BF16),
        in_specs=[ANY],
        out_specs=VMEM,
        scratch_shapes=[pltpu.SemaphoreType.DMA(())],
        cost_estimate=pl.CostEstimate(
            flops=0, transcendentals=0, bytes_accessed=4 * ready * rows * span
        ),
        compiler_params=pltpu.CompilerParams(vmem_limit_bytes=44 << 20),
        name="fetch",
    )(cholesky)
    partial = pl.pallas_call(
        lambda *refs: pair_sums(*refs, step=step),
        out_shape=jax.ShapeDtypeStruct((nvec, active, active), BF16),
        in_specs=[VMEM, ANY, VMEM, VMEM, VMEM],
        out_specs=VMEM,
        scratch_shapes=[
            pltpu.VMEM((nvec - ready, rows, span), BF16),
            pltpu.VMEM((span, active), BF16),
            pltpu.SemaphoreType.DMA((nvec // step,)),
        ],
        compiler_params=pltpu.CompilerParams(vmem_limit_bytes=44 << 20),
        name="pair_sums",
    )(early, cholesky, mine, other, coeffs)

    partial = partial.reshape(nvec, auxes, aos, active)
    arrived = exchange(partial.transpose(2, 1, 0, 3), "ao")
    done = arrived.astype(F32).sum(axis=0).astype(BF16)

    left = jnp.broadcast_to(done[:, None], (auxes, aos, nvec, active))
    cols = done.reshape(auxes, nvec, aos, width).transpose(2, 0, 3, 1)
    cols = cols.reshape(1, aos, -1, active)
    cols = jnp.pad(cols, ((0, 0), (0, 0), (0, 8 - cols.shape[2]), (0, 0)))
    cols = jnp.broadcast_to(cols, (auxes, *cols.shape[1:]))
    sent = jnp.concatenate([left, cols], axis=2)
    got = exchange(sent.reshape(auxes * aos, nvec + 8, active), ("aux", "ao"))
    right = got[:, nvec:].reshape(auxes, aos, -1)[:, :, : auxes * width * nvec]
    right = right.reshape(auxes, aos, auxes, width, nvec).transpose(0, 4, 3, 2, 1)
    right = right.reshape(auxes * nvec, width * active)
    count = 8
    return pl.pallas_call(
        products,
        grid=(band // count,),
        out_shape=jax.ShapeDtypeStruct((band * active, width * active), F32),
        in_specs=[
            pl.BlockSpec((auxes, count, nvec + 8, active), lambda g: (0, g, 0, 0)),
            pl.BlockSpec((auxes * nvec, width * active), lambda g: (0, 0)),
        ],
        out_specs=pl.BlockSpec((count * active, width * active), lambda g: (g, 0)),
        compiler_params=pltpu.CompilerParams(vmem_limit_bytes=24 << 20),
        name="products",
    )(got.reshape(auxes, aos, nvec + 8, active), right)


def solution(mesh):
    in_specs = (P("aux", "ao", None), P("ao", None))
    out_specs = P("aux", "ao")
    return jax.shard_map(
        on_device, mesh=mesh, in_specs=in_specs, out_specs=out_specs, check_vma=False
    )
```

time: 109 us -> 78.4 us (0.72)
  waiting for transfers between devices: 24.8 us -> 0.01 us
  matrix products: 13.2 us -> 0 us
  Pallas kernels: 0 us -> 11.7 us
  starting transfers between devices: 7.97 us -> 2.15 us
  blocking collectives: 58.9 us -> 61.4 us
    all_to_all x1 -> x0, waiting for transfers between devices: 24.8 us -> none  [from_everyone(): return lax.all_to_all(copies, axis, split_axis=0, concat_axis=0, tiled=True)]
    dot_general x3 -> x0, matrix products: 13.2 us -> none  [the longest x1 8.19 us: on_device(): jnp.dot(flat_rows, gather_directly(coeffs, 'ao', 0), preferred_element_ty...]
    pallas_call x0 -> x3, Pallas kernels: none -> 11.7 us  [the longest x1 5.06 us: on_device(): pl.pallas_call(lambda *refs: pair_sums(*refs, step=step), out_shape=jax.S...]
    all_to_all x1 -> x0, starting transfers between devices: 7.97 us -> none  [from_everyone(): return lax.all_to_all(copies, axis, split_axis=0, concat_axis=0, tiled=True)]
    broadcast_in_dim x3 -> x5, local copies, waits for them, and re-layouts: 2.98 us -> 0.39 us  [the longest x3 0.21 us: on_device(): cols = jnp.broadcast_to(cols, (auxes, *cols.shape[1:]))]
    all_to_all x3, blocking collectives: 58.9 us -> 61.4 us  [exchange(): return lax.all_to_all(blocks, axes, split_axis=0, concat_axis=0, tiled=True)]
    ppermute x0 -> x1, starting transfers between devices: none -> 2.15 us  [on_device(): other = lax.ppermute(mine, 'aux', [(a, a ^ 1) for a in range(auxes)])]
  transfers between devices with their start and end apart: 1 -> 1, of which waited for: 1 -> 0; matrix products, arithmetic and copies ran while one was open for 0% -> 0% of each run, Pallas kernels for 0% -> 3%
where the time goes in v1:
time: 78.4 us; the launch traced here: 78.1 us
  blocking collectives  61.4 us (78%)
  Pallas kernels  11.7 us (15%)
  local copies, waits for them, and re-layouts  2.4 us (3%)
  starting transfers between devices  2.15 us (3%)
    all_to_all x3, blocking collectives, exchange(): return lax.all_to_all(blocks, axes, split_axis=0, concat_axis=0, tiled=True)  61.4 us
    pallas_call x1, Pallas kernels, on_device(): pl.pallas_call(lambda *refs: pair_sums(*refs, step=step), out_shape=jax.S...  5.06 us
    pallas_call x1, Pallas kernels, on_device(): pl.pallas_call(products, grid=(band // count,), out_shape=jax.ShapeDtypeS...  4.31 us
    pallas_call x1, Pallas kernels, on_device(): pl.pallas_call(fetch, out_shape=jax.ShapeDtypeStruct((ready, rows, span),...  2.34 us
    ppermute x1, starting transfers between devices, on_device(): other = lax.ppermute(mine, 'aux', [(a, a ^ 1) for a in range(auxes)])  2.15 us
  transfers between devices with their start and end apart: 1, of which 0 were waited for; matrix products, arithmetic and copies ran while one was open for 0% of the time, Pallas kernels for 3%

profile of v1, /device:TPU:1, one launch (start us, length us, event | category | flops | bytes accessed | tf_op | source)
XLA Modules:
  0.0 78.1 jit_solution(3133171300880307676)
XLA Ops:
  0.0 0.7 constant_dynamic-slice_fusion
  0.7 0.1 broadcast_in_dim.16
  0.8 23.7 %all_to_all.15.refs_2_ = bf16[32,64,128]{2,1,0:T(8,128)(2,1)S(1)} all-to-all(bf16[32,64,128]{2,1,0:T(8,128)(2,1)S(1)} %broadcast_in_dim.16), channel_id=1, replica_groups=mesh['aux'=4,'ao'=32] {'ao'}, dimensions={0} | all-to-all | bytes 1048576 | tf_op jit(solution)/shard_map/all_to_all | solution.py:14
  24.5 0.0 copy-start
  24.5 2.1 %collective-permute-start = (bf16[32,64,128]{2,1,0:T(8,128)(2,1)S(1)}, bf16[32,64,128]{2,1,0:T(8,128)(2,1)S(1)}, u32[]{:S(2)}, u32[]{:S(2)}) collective-permute-start(bf16[32,64,128]{2,1,0:T(8,128)(2,1)S(1)} %all_to_all.15.refs_2_), channel_id=1, source_target_pairs={{0,32},{32,0},{64,96},{96,64},{1,33},{33,1},{65,97},{97,65},{2,34}... | collective-permute-start | bytes 1572872 | tf_op jit(solution)/shard_map/ppermute | solution.py:115
  26.7 2.3 %fetch.1.refs_0_ = bf16[8,128,2304]{2,1,0:T(8,128)(2,1)S(1)} custom-call(bf16[16,128,4096]{2,1,0:T(8,128)(2,1)} %refs_1_.1), custom_call_target="tpu_custom_call" | custom-call | bytes 9437184 | tf_op jit(solution)/shard_map/fetch/pallas_call | solution.py:117
  29.0 0.0 collective-permute-done.refs_3_
  29.0 0.0 copy-done
  29.0 5.1 %pair_sums.1 = bf16[16,128,128]{2,1,0:T(8,128)(2,1)S(1)} custom-call(bf16[8,128,2304]{2,1,0:T(8,128)(2,1)S(1)} %fetch.1.refs_0_, bf16[16,128,4096]{2,1,0:T(8,128)(2,1)} %refs_1_.1, bf16[32,64,128]{2,1,0:T(8,128)(2,1)S(1)} %all_to_all.15.refs_2_, bf16[32,64,128]{2,1,0:T(8,128)(2,1)S(1)} %collective-permute-done.refs_3_, bf16[128,128]{1,0:T(8,128)(2,1)S(1)} %copy-done), custom_call_target="tpu_custom_call" | custom-call | tf_op jit(solution)/shard_map/pair_sums/pallas_call | solution.py:129
  34.1 0.3 copy.23
  34.4 16.5 %all_to_all.16 = bf16[32,4,16,128]{3,1,2,0:T(4,128)(2,1)S(1)} all-to-all(bf16[32,4,16,128]{3,1,2,0:T(4,128)(2,1)S(1)} %bitcast.18), channel_id=1, replica_groups=mesh['aux'=4,'ao'=32] {'ao'}, dimensions={0} | all-to-all | bytes 1048576 | tf_op jit(solution)/shard_map/all_to_all | solution.py:14
  50.9 0.2 reduce_sum.12
  51.1 0.1 copy.16
  51.3 0.1 copy.17
  51.5 0.1 copy.18
  51.6 0.1 broadcast_in_dim.17
  51.7 0.1 pad_maximum_fusion
  51.9 21.2 %all_to_all.17 = bf16[128,24,128]{2,1,0:T(8,128)(2,1)S(1)} all-to-all(bf16[128,24,128]{2,1,0:T(8,128)(2,1)S(1)} %bitcast.17), channel_id=1, replica_groups=mesh['aux'=4,'ao'=32] {'aux','ao'}, dimensions={0} | all-to-all | bytes 1572864 | tf_op jit(solution)/shard_map/all_to_all | solution.py:14
  73.1 0.1 reshape.30
  73.2 0.2 copy.19
  73.4 0.2 copy.20
  73.6 0.2 reshape.32.right_ref
  73.8 4.3 %products.1 = f32[4096,512]{1,0:T(8,128)} custom-call(bf16[4,32,24,128]{3,2,1,0:T(8,128)(2,1)S(1)} %bitcast.15, bf16[64,512]{1,0:T(8,128)(2,1)S(1)} %reshape.32.right_ref), custom_call_target="tpu_custom_call" | custom-call | tf_op jit(solution)/shard_map/products/pallas_call | solution.py:158
  (5 shorter events, 0.1 us)
Async XLA Ops:
  24.5 4.5 %copy-start = (bf16[128,128]{1,0:T(8,128)(2,1)S(1)}, bf16[128,128]{1,0:T(8,128)(2,1)}, u32[]{:S(2)}) copy-start(bf16[128,128]{1,0:T(8,128)(2,1)} %refs_4_.1) | copy-start | bytes 98308
  24.5 4.5 %collective-permute-start = (bf16[32,64,128]{2,1,0:T(8,128)(2,1)S(1)}, bf16[32,64,128]{2,1,0:T(8,128)(2,1)S(1)}, u32[]{:S(2)}, u32[]{:S(2)}) collective-permute-start(bf16[32,64,128]{2,1,0:T(8,128)(2,1)S(1)} %all_to_all.15.refs_2_), channel_id=1, source_target_pairs={{0,32},{32,0},{64,96},{96,64},{1,33},{33,1},{65,97},{97,65},{2,34}... | collective-permute-start | bytes 1572872 | tf_op jit(solution)/shard_map/ppermute | solution.py:115

commit v2 on v1

--- a/solution.py
+++ b/solution.py
@@ -45,7 +45,7 @@
 
 
 def pair_sums(
-    early_ref, chol_ref, mine_ref, other_ref, coeffs_ref, out_ref, held_ref, near_ref, sems, *, step
+    early_ref, chol_ref, mine_ref, other_ref, coeffs_ref, out_ref, held_ref, near_ref, sems, *, step, ahead
 ):
     ready, rows, span = early_ref.shape
     nvec = ready + held_ref.shape[0]
@@ -57,8 +57,12 @@
     def late(first):
         return held_ref.at[pl.ds(first - ready, step)]
 
-    for first in range(ready, nvec, step):
-        start_window(chol_ref.at[pl.ds(first, step)], late(first), sems.at[first // step])
+    def begin(first):
+        if first < nvec:
+            start_window(chol_ref.at[pl.ds(first, step)], late(first), sems.at[first // step])
+
+    for first in range(ready, ready + ahead, step):
+        begin(first)
     for t in range(steps):
         for s in range(2):
             block = lax.rem(at + t, wides) * 2 + s
@@ -84,6 +88,7 @@
             slab = early_ref[first : first + step]
         else:
             wait_window(late(first), sems.at[first // step])
+            begin(first + ahead)
             slab = late(first)[...]
         slab = slab.reshape(step * rows, span)
         half = jnp.dot(slab, near, preferred_element_type=F32).astype(BF16)
@@ -93,14 +98,48 @@
     finish(*before)
 
 
-def products(left_ref, right_ref, out_ref):
-    auxes, count, deep, active = left_ref.shape
+def products(got_ref, out_ref, right_ref, held_ref, sems):
+    auxes, aos, pieces, pair, active = got_ref.shape
     nvec = right_ref.shape[0] // auxes
-    for k in range(count):
-        left = jnp.concatenate([left_ref[a, k, :nvec, :] for a in range(auxes)], axis=0)
-        out_ref[k * active : (k + 1) * active, :] = lax.dot_general(
-            left, right_ref[...], (((0,), (0,)), ((), ())), preferred_element_type=F32
+    deep = nvec // pair
+    width = right_ref.shape[1] // active
+    part = width * nvec
+    slots, size = held_ref.shape[:2]
+    count = size // active
+
+    for a in range(auxes):
+        cols = []
+        for piece in range(deep, pieces):
+            both = got_ref[a, :, piece].astype(F32)
+            for s in range(pair):
+                row = both[:, s, :]
+                cols += [row[:, c : c + part] for c in range(0, active, part)]
+        turned = jnp.concatenate(cols, axis=0).T.astype(BF16)
+        for v in range(width):
+            right_ref[a * nvec : (a + 1) * nvec, v * active : (v + 1) * active] = turned[
+                v * nvec : (v + 1) * nvec
+            ]
+    right = right_ref[...]
+
+    def write(g):
+        slot = g % slots
+        return pltpu.make_async_copy(
+            held_ref.at[slot], out_ref.at[pl.ds(g * size, size)], sems.at[slot]
         )
+
+    groups = aos // count
+    for g in range(groups):
+        if g >= slots:
+            write(g - slots).wait()
+        for k in range(count):
+            left = [got_ref[a, g * count + k, :deep].reshape(nvec, active) for a in range(auxes)]
+            left = jnp.concatenate(left, axis=0)
+            held_ref[g % slots, k * active : (k + 1) * active, :] = lax.dot_general(
+                left, right, (((0,), (0,)), ((), ())), preferred_element_type=F32
+            )
+        write(g).start()
+    for g in range(groups - slots, groups):
+        write(g).wait()
 
 
 def on_device(cholesky, coeffs):
@@ -113,7 +152,7 @@
     own = lax.dynamic_slice_in_dim(coeffs, core * (rows // 2), rows // 2, 0)
     mine = exchange(jnp.broadcast_to(own, (aos, rows // 2, active)), "ao")
     other = lax.ppermute(mine, "aux", [(a, a ^ 1) for a in range(auxes)])
-    span, ready, step = (aos // 4 + 1) * 2 * rows, nvec // 2, 2
+    span, ready, step, ahead = (aos // 4 + 1) * 2 * rows, 4, 2, 6
     early = pl.pallas_call(
         fetch,
         out_shape=jax.ShapeDtypeStruct((ready, rows, span), BF16),
@@ -127,7 +166,7 @@
         name="fetch",
     )(cholesky)
     partial = pl.pallas_call(
-        lambda *refs: pair_sums(*refs, step=step),
+        lambda *refs: pair_sums(*refs, step=step, ahead=ahead),
         out_shape=jax.ShapeDtypeStruct((nvec, active, active), BF16),
         in_specs=[VMEM, ANY, VMEM, VMEM, VMEM],
         out_specs=VMEM,
@@ -144,29 +183,31 @@
     arrived = exchange(partial.transpose(2, 1, 0, 3), "ao")
     done = arrived.astype(F32).sum(axis=0).astype(BF16)
 
-    left = jnp.broadcast_to(done[:, None], (auxes, aos, nvec, active))
+    extra = auxes * width * nvec // (2 * active)
+    left = done.reshape(auxes, 1, nvec // 2, 2, active)
+    left = jnp.pad(left, ((0, 0), (0, 0), (0, extra), (0, 0), (0, 0)))
+    sent = jnp.broadcast_to(left, (auxes, aos, nvec // 2 + extra, 2, active))
     cols = done.reshape(auxes, nvec, aos, width).transpose(2, 0, 3, 1)
-    cols = cols.reshape(1, aos, -1, active)
-    cols = jnp.pad(cols, ((0, 0), (0, 0), (0, 8 - cols.shape[2]), (0, 0)))
-    cols = jnp.broadcast_to(cols, (auxes, *cols.shape[1:]))
-    sent = jnp.concatenate([left, cols], axis=2)
-    got = exchange(sent.reshape(auxes * aos, nvec + 8, active), ("aux", "ao"))
-    right = got[:, nvec:].reshape(auxes, aos, -1)[:, :, : auxes * width * nvec]
-    right = right.reshape(auxes, aos, auxes, width, nvec).transpose(0, 4, 3, 2, 1)
-    right = right.reshape(auxes * nvec, width * active)
-    count = 8
+    cols = jnp.broadcast_to(
+        cols.reshape(1, aos, extra, 2, active), (auxes, aos, extra, 2, active)
+    )
+    sent = lax.dynamic_update_slice(sent, cols, (0, 0, nvec // 2, 0, 0))
+    got = exchange(sent.reshape(auxes * aos, nvec // 2 + extra, 2, active), ("aux", "ao"))
+    got = got.reshape(auxes, aos, nvec // 2 + extra, 2, active)
+    count, slots = 4, 4
     return pl.pallas_call(
         products,
-        grid=(band // count,),
         out_shape=jax.ShapeDtypeStruct((band * active, width * active), F32),
-        in_specs=[
-            pl.BlockSpec((auxes, count, nvec + 8, active), lambda g: (0, g, 0, 0)),
-            pl.BlockSpec((auxes * nvec, width * active), lambda g: (0, 0)),
+        in_specs=[VMEM],
+        out_specs=ANY,
+        scratch_shapes=[
+            pltpu.VMEM((auxes * nvec, width * active), BF16),
+            pltpu.VMEM((slots, count * active, width * active), F32),
+            pltpu.SemaphoreType.DMA((slots,)),
         ],
-        out_specs=pl.BlockSpec((count * active, width * active), lambda g: (g, 0)),
         compiler_params=pltpu.CompilerParams(vmem_limit_bytes=24 << 20),
         name="products",
-    )(got.reshape(auxes, aos, nvec + 8, active), right)
+    )(got)
 
 
 def solution(mesh):

time: 78.4 us -> 74.8 us (0.954)
  blocking collectives: 61.4 us -> 59.6 us
  Pallas kernels: 11.7 us -> 10.6 us
    all_to_all x3, blocking collectives: 61.4 us -> 59.6 us  [exchange(): return lax.all_to_all(blocks, axes, split_axis=0, concat_axis=0, tiled=True)]
  transfers between devices with their start and end apart: 1 -> 1, of which waited for: 0 -> 0; matrix products, arithmetic and copies ran while one was open for 0% -> 0% of each run, Pallas kernels for 3% -> 2%
where the time goes in v2:
time: 74.8 us; the launch traced here: 74.5 us
  blocking collectives  59.6 us (80%)
  Pallas kernels  10.6 us (14%)
  starting transfers between devices  2.15 us (3%)
  local copies, waits for them, and re-layouts  1.87 us (2%)
    all_to_all x3, blocking collectives, exchange(): return lax.all_to_all(blocks, axes, split_axis=0, concat_axis=0, tiled=True)  59.6 us
    pallas_call x1, Pallas kernels, on_device(): pl.pallas_call(lambda *refs: pair_sums(*refs, step=step, ahead=ahead), ou...  5.02 us
    pallas_call x1, Pallas kernels, on_device(): pl.pallas_call(products, out_shape=jax.ShapeDtypeStruct((band * active, w...  3.87 us
    ppermute x1, starting transfers between devices, on_device(): other = lax.ppermute(mine, 'aux', [(a, a ^ 1) for a in range(auxes)])  2.15 us
    pallas_call x1, Pallas kernels, on_device(): pl.pallas_call(fetch, out_shape=jax.ShapeDtypeStruct((ready, rows, span),...  1.67 us
  transfers between devices with their start and end apart: 1, of which 0 were waited for; matrix products, arithmetic and copies ran while one was open for 0% of the time, Pallas kernels for 2%

profile of v2, /device:TPU:1, one launch (start us, length us, event | category | flops | bytes accessed | tf_op | source)
XLA Modules:
  0.0 74.5 jit_solution(13007893307562054920)
XLA Ops:
  0.0 0.7 constant_dynamic-slice_fusion
  0.7 0.1 broadcast_in_dim.17
  0.8 23.7 %all_to_all.15.refs_2_ = bf16[32,64,128]{2,1,0:T(8,128)(2,1)S(1)} all-to-all(bf16[32,64,128]{2,1,0:T(8,128)(2,1)S(1)} %broadcast_in_dim.17), channel_id=1, replica_groups=mesh['aux'=4,'ao'=32] {'ao'}, dimensions={0} | all-to-all | bytes 1048576 | tf_op jit(solution)/shard_map/all_to_all | solution.py:14
  24.5 0.0 copy-start
  24.5 2.1 %collective-permute-start = (bf16[32,64,128]{2,1,0:T(8,128)(2,1)S(1)}, bf16[32,64,128]{2,1,0:T(8,128)(2,1)S(1)}, u32[]{:S(2)}, u32[]{:S(2)}) collective-permute-start(bf16[32,64,128]{2,1,0:T(8,128)(2,1)S(1)} %all_to_all.15.refs_2_), channel_id=1, source_target_pairs={{0,32},{32,0},{64,96},{96,64},{1,33},{33,1},{65,97},{97,65},{2,34}... | collective-permute-start | bytes 1572872 | tf_op jit(solution)/shard_map/ppermute | solution.py:154
  26.7 1.7 %fetch.1.refs_0_ = bf16[4,128,2304]{2,1,0:T(8,128)(2,1)S(1)} custom-call(bf16[16,128,4096]{2,1,0:T(8,128)(2,1)} %refs_1_.1), custom_call_target="tpu_custom_call" | custom-call | bytes 4718592 | tf_op jit(solution)/shard_map/fetch/pallas_call | solution.py:156
  28.3 0.0 collective-permute-done.refs_3_
  28.4 0.0 copy-done
  28.4 5.0 %pair_sums.1 = bf16[16,128,128]{2,1,0:T(8,128)(2,1)S(1)} custom-call(bf16[4,128,2304]{2,1,0:T(8,128)(2,1)S(1)} %fetch.1.refs_0_, bf16[16,128,4096]{2,1,0:T(8,128)(2,1)} %refs_1_.1, bf16[32,64,128]{2,1,0:T(8,128)(2,1)S(1)} %all_to_all.15.refs_2_, bf16[32,64,128]{2,1,0:T(8,128)(2,1)S(1)} %collective-permute-done.refs_3_, bf16[128,128]{1,0:T(8,128)(2,1)S(1)} %copy-done), custom_call_target="tpu_custom_call" | custom-call | tf_op jit(solution)/shard_map/pair_sums/pallas_call | solution.py:168
  33.4 0.3 copy.17
  33.7 16.6 %all_to_all.16 = bf16[32,4,16,128]{3,1,2,0:T(4,128)(2,1)S(1)} all-to-all(bf16[32,4,16,128]{3,1,2,0:T(4,128)(2,1)S(1)} %bitcast.16), channel_id=1, replica_groups=mesh['aux'=4,'ao'=32] {'ao'}, dimensions={0} | all-to-all | bytes 1048576 | tf_op jit(solution)/shard_map/all_to_all | solution.py:14
  50.3 0.2 reduce_sum.12
  50.5 0.1 copy.12
  50.7 0.1 copy.13
  50.8 0.1 copy.14
  50.9 0.3 broadcast_in_dim.19
  51.2 0.1 broadcast_dynamic-update-slice_fusion
  51.3 19.4 %all_to_all.17 = bf16[128,9,2,128]{3,2,1,0:T(2,128)(2,1)S(1)} all-to-all(bf16[128,9,2,128]{3,2,1,0:T(2,128)(2,1)S(1)} %bitcast.15), channel_id=1, replica_groups=mesh['aux'=4,'ao'=32] {'aux','ao'}, dimensions={0} | all-to-all | bytes 1179648 | tf_op jit(solution)/shard_map/all_to_all | solution.py:14
  70.7 3.9 %products.1 = f32[4096,512]{1,0:T(8,128)} custom-call(bf16[4,32,9,2,128]{4,3,2,1,0:T(2,128)(2,1)S(1)} %bitcast.13), custom_call_target="tpu_custom_call" | custom-call | tf_op jit(solution)/shard_map/products/pallas_call | solution.py:198
  (2 shorter events, 0.0 us)
Async XLA Ops:
  24.5 3.8 %copy-start = (bf16[128,128]{1,0:T(8,128)(2,1)S(1)}, bf16[128,128]{1,0:T(8,128)(2,1)}, u32[]{:S(2)}) copy-start(bf16[128,128]{1,0:T(8,128)(2,1)} %refs_4_.1) | copy-start | bytes 98308
  24.5 3.8 %collective-permute-start = (bf16[32,64,128]{2,1,0:T(8,128)(2,1)S(1)}, bf16[32,64,128]{2,1,0:T(8,128)(2,1)S(1)}, u32[]{:S(2)}, u32[]{:S(2)}) collective-permute-start(bf16[32,64,128]{2,1,0:T(8,128)(2,1)S(1)} %all_to_all.15.refs_2_), channel_id=1, source_target_pairs={{0,32},{32,0},{64,96},{96,64},{1,33},{33,1},{65,97},{97,65},{2,34}... | collective-permute-start | bytes 1572872 | tf_op jit(solution)/shard_map/ppermute | solution.py:154
